TPU v7x, 32 devices: a whole 2x2x4 slice. The times are simulated.
32 devices in a mesh: face: 8 (over y, x, core), member: 4 (over z).
Axes of the slice: x: 2, y: 2, z: 4, core: 2. Of those that a mesh axis runs over, the one named last changes fastest.
Arguments:
- features: bfloat16 [8, 48, 16, 16, 256], P('member', 'face'), may hold values from -6 to 6
- observed: bfloat16 [48, 80, 256], P('face', None, 'member'), may hold values from -6 to 6
- conv_weights: bfloat16 [2304, 2, 256], P(('face', 'member')), may hold values from -0.125 to 0.125
- head_weight: bfloat16 [256, 80], P(('face', 'member')), may hold values from -0.375 to 0.375
- adjacency: int32 [48, 4, 3], replicated, may hold values from 0 to 47, as said below
- placement_map: int32 [48], replicated, may hold values from 0 to 47, each once
Outputs:
- conv_grads: float32 [2304, 2, 256], P(('face', 'member'))
- head_grad: float32 [256, 80], P(('face', 'member'))
Inputs may be any that keep to these rules, and one draw needn't show every extreme that they name: `adjacency`: the table is the gluing of the 12 HEALPix base faces, each cut into 4 square tiles, under a labelling of the tiles drawn from the seed: entry [t, a] = (n, b, f) glues side a of tile t to side b of tile n, reversed when f is 1; the gluing is mutual (entry [n, b] is (t, a, f)) and never joins a side to itself. `placement_map`: each tile stands at exactly one slot.
All inputs are finite; a program needn't handle non-finite values.
Results may differ from a plain program's by a relative error of at most 0.0005.
Values may be sent and summed in bfloat16 or wider, within the bound.
A program may use at most 128 MiB of HBM per device.

v0:
```python
import jax
import jax.numpy as jnp
from jax import lax
from jax.sharding import PartitionSpec as P

smooth_sq = 0.0625


def split_edges(grid_field):
    return jnp.stack(
        [
            grid_field[:, :, 0],
            grid_field[:, :, :, -1],
            grid_field[:, :, -1],
            grid_field[:, :, :, 0],
        ],
        axis=2,
    )


def border_of(padded):
    return jnp.stack(
        [
            padded[:, :, 0, 1:-1],
            padded[:, :, 1:-1, -1],
            padded[:, :, -1, 1:-1],
            padded[:, :, 1:-1, 0],
        ],
        axis=2,
    )


def surround(grid_field, border):
    ensemble_members, tile_count, height, tile_w, channels = grid_field.shape
    corner = jnp.zeros((ensemble_members, tile_count, 1, 1, channels), grid_field.dtype)
    top_row = jnp.concatenate([corner, border[:, :, 0][:, :, None], corner], axis=3)
    low_row = jnp.concatenate([corner, border[:, :, 2][:, :, None], corner], axis=3)
    middle = jnp.concatenate(
        [border[:, :, 3][:, :, :, None], grid_field, border[:, :, 1][:, :, :, None]], axis=3
    )
    return jnp.concatenate([top_row, middle, low_row], axis=2)


def convolve(padded, weight):
    channels = weight.shape[1]
    height = padded.shape[2] - 2
    tile_w = padded.shape[3] - 2
    summed = None
    for tap_index in range(9):
        row_off, col_off = divmod(tap_index, 3)
        window = padded[:, :, row_off : row_off + height, col_off : col_off + tile_w, :]
        product_part = jnp.dot(
            window.reshape(-1, channels),
            weight[tap_index * channels : (tap_index + 1) * channels],
            preferred_element_type=jnp.float32,
        )
        summed = product_part if summed is None else summed + product_part
    return summed.reshape(padded.shape[:2] + (height, tile_w, channels))


def transpose_conv(slope_in, weight):
    channels = weight.shape[1]
    ensemble_members, tile_count, height, tile_w, _ = slope_in.shape
    result = jnp.zeros(
        (ensemble_members, tile_count, height + 2, tile_w + 2, channels), jnp.float32
    )
    flat_slope = slope_in.reshape(-1, channels)
    for tap_index in range(9):
        row_off, col_off = divmod(tap_index, 3)
        product_part = lax.dot_general(
            flat_slope,
            weight[tap_index * channels : (tap_index + 1) * channels],
            (((1,), (1,)), ((), ())),
            preferred_element_type=jnp.float32,
        )
        result = result.at[:, :, row_off : row_off + height, col_off : col_off + tile_w, :].add(
            product_part.reshape(slope_in.shape)
        )
    return result


def weight_slope(padded, slope_in):
    channels = slope_in.shape[-1]
    height = slope_in.shape[2]
    tile_w = slope_in.shape[3]
    flat_slope = slope_in.reshape(-1, channels)
    pieces_out = []
    for tap_index in range(9):
        row_off, col_off = divmod(tap_index, 3)
        window = padded[:, :, row_off : row_off + height, col_off : col_off + tile_w, :]
        pieces_out.append(
            lax.dot_general(
                window.reshape(-1, channels),
                flat_slope,
                (((0,), (0,)), ((), ())),
                preferred_element_type=jnp.float32,
            )
        )
    return jnp.concatenate(pieces_out, axis=0)


def dsilu(argument):
    sigmoid_v = jax.nn.sigmoid(argument)
    return sigmoid_v * (1.0 + argument * (1.0 - sigmoid_v))


def partner_table(adjacency, placement_map, first_slot, tile_dev):
    tile_count = placement_map.shape[0]
    slot_ids = jnp.arange(tile_count, dtype=jnp.int32)
    my_slots = first_slot + jnp.arange(tile_dev, dtype=jnp.int32)
    slot_hit = (slot_ids[None, :] == my_slots[:, None]).astype(jnp.int32)
    my_tiles = jnp.sum(slot_hit * placement_map[None, :], axis=1)
    tile_hit = (slot_ids[None, :] == my_tiles[:, None]).astype(jnp.int32)
    entries = jnp.sum(tile_hit[:, :, None, None] * adjacency[None], axis=1)
    slot_of = jnp.sum(
        slot_ids[:, None] * (placement_map[:, None] == slot_ids[None, :]).astype(jnp.int32), axis=0
    )
    source_slot = jnp.sum(
        (slot_ids[None, None, :] == entries[:, :, 0][:, :, None]).astype(jnp.int32)
        * slot_of[None, None, :],
        axis=2,
    )
    source_index = source_slot * 4 + entries[:, :, 1]
    edge_ids = jnp.arange(tile_count * 4, dtype=jnp.int32)
    selector = (edge_ids[None, None, :] == source_index[:, :, None]).astype(jnp.bfloat16)
    return (selector, entries[:, :, 2])


def fetch_rims(gathered, selector, flip_flags, tile_dev):
    ensemble_members, tile_count, side_count, length, channels = gathered.shape
    flattened = gathered.reshape(ensemble_members, tile_count * side_count, length * channels)
    fetched = jnp.einsum("abe,mef->mabf", selector, flattened, preferred_element_type=jnp.float32)
    fetched = fetched.astype(jnp.bfloat16).reshape(
        ensemble_members, tile_dev, side_count, length, channels
    )
    return jnp.where(flip_flags[None, :, :, None, None] == 1, fetched[:, :, :, ::-1, :], fetched)


def score_slope(local_vals, all_vals, obs_vals, height):
    ensemble_members = all_vals.shape[0]
    spread = local_vals[:, None] - all_vals[None]
    paired = jnp.sum(spread * lax.rsqrt(spread * spread + smooth_sq), axis=1)
    own_gap = local_vals - obs_vals[None]
    return (
        own_gap * lax.rsqrt(own_gap * own_gap + smooth_sq) / ensemble_members
        - paired / (ensemble_members * ensemble_members)
    ) / height


def shards(features, observed, conv_weights, head_weight, adjacency, placement_map):
    members, tile_dev, height, tile_w, channels = features.shape
    full_weights, full_head = (
        lax.all_gather(conv_weights, ("face", "member"), axis=0, tiled=True),
        lax.all_gather(head_weight, ("face", "member"), axis=0, tiled=True),
    )
    selector, flip_flags = partner_table(
        adjacency, placement_map, lax.axis_index("face") * tile_dev, tile_dev
    )
    feature_edges = lax.all_gather(split_edges(features), "face", axis=1, tiled=True)
    pad_in = surround(features, fetch_rims(feature_edges, selector, flip_flags, tile_dev))
    pre_one = convolve(pad_in, full_weights[:, 0, :])
    act_one = jax.nn.silu(pre_one).astype(jnp.bfloat16)
    hidden_edges = lax.all_gather(split_edges(act_one), "face", axis=1, tiled=True)
    pad_mid = surround(act_one, fetch_rims(hidden_edges, selector, flip_flags, tile_dev))
    pre_two = convolve(pad_mid, full_weights[:, 1, :])
    act_two = jax.nn.silu(pre_two).astype(jnp.bfloat16)
    flat_two = act_two.reshape(members, tile_dev, height * tile_w, channels)
    outputs = jnp.einsum(
        "mtpc,cv->mtvp", flat_two, full_head, preferred_element_type=jnp.float32
    ).astype(jnp.bfloat16)
    by_pixel = lax.all_to_all(outputs, "member", split_axis=3, concat_axis=0, tiled=True)
    pixel_vals = by_pixel.astype(jnp.float32)
    slope_cells = score_slope(pixel_vals, pixel_vals, observed.astype(jnp.float32), height).astype(
        jnp.bfloat16
    )
    slope_out = lax.all_to_all(slope_cells, "member", split_axis=0, concat_axis=3, tiled=True)
    head_term = jnp.einsum("mtpc,mtvp->cv", flat_two, slope_out, preferred_element_type=jnp.float32)
    back_two = jnp.einsum("mtvp,cv->mtpc", slope_out, full_head, preferred_element_type=jnp.float32)
    back_two = back_two.reshape(members, tile_dev, height, tile_w, channels)
    slope_two = (back_two * dsilu(pre_two)).astype(jnp.bfloat16)
    grad_two = weight_slope(pad_mid, slope_two)
    late_shard, head_shard = (
        lax.psum_scatter(grad_two, ("face", "member"), scatter_dimension=0, tiled=True),
        lax.psum_scatter(head_term, ("face", "member"), scatter_dimension=0, tiled=True),
    )
    pad_slope = transpose_conv(slope_two, full_weights[:, 1, :]).astype(jnp.bfloat16)
    rim_edges = lax.all_gather(border_of(pad_slope), "face", axis=1, tiled=True)
    returned = fetch_rims(rim_edges, selector, flip_flags, tile_dev).astype(jnp.float32)
    slope_mid = pad_slope[:, :, 1:-1, 1:-1].astype(jnp.float32)
    slope_mid = slope_mid.at[:, :, 0].add(returned[:, :, 0])
    slope_mid = slope_mid.at[:, :, :, -1].add(returned[:, :, 1])
    slope_mid = slope_mid.at[:, :, -1].add(returned[:, :, 2])
    slope_mid = slope_mid.at[:, :, :, 0].add(returned[:, :, 3])
    slope_one = (slope_mid * dsilu(pre_one)).astype(jnp.bfloat16)
    grad_one = weight_slope(pad_in, slope_one)
    early_shard = lax.psum_scatter(grad_one, ("face", "member"), scatter_dimension=0, tiled=True)
    conv_shard = jnp.stack([early_shard, late_shard], axis=1)
    return (conv_shard, head_shard)


def solution(mesh):
    in_specs = (
        P("member", "face", None, None, None),
        P("face", None, "member"),
        P(("face", "member"), None, None),
        P(("face", "member"), None),
        P(),
        P(),
    )
    out_specs = (P(("face", "member"), None, None), P(("face", "member"), None))
    return jax.shard_map(shards, mesh=mesh, in_specs=in_specs, out_specs=out_specs, check_vma=False)
```

profile of v0, /device:TPU:0, one launch (start us, length us, event | category | flops | bytes accessed | tf_op | source)
XLA Modules:
  0.0 850.0 jit_solution(15067462551593991296)
XLA Ops:
  7.2 1.8 fusion.111
  13.3 32.6 %all-gather.5.cloned.1.call-done = bf16[2,48,4,16,256]{4,3,1,0,2:T(8,128)(2,1)} async-done(((bf16[2,6,4,16,256]{4,3,1,0,2:T(8,128)(2,1)}), bf16[2,48,4,16,256]{4,3,1,0,2:T(8,128)(2,1)}) %all-gather.5.cloned.1.call-update) | async-done | bytes 3145744 | tf_op jit(solution)/shard_map/all_gather | solution.py:159
  45.9 2.3 copy.300
  48.3 3.4 reshape.811
  51.7 2.6 fusion.3
  57.0 2.9 pad_maximum_fusion.4
  60.0 3.6 pad_maximum_fusion
  63.6 3.6 fusion.108
  67.3 3.2 fusion.107
  70.5 36.2 %all-gather.7.cloned.1.call-done = bf16[2304,2,256]{2,0,1:T(8,128)(2,1)} async-done(((bf16[72,2,256]{2,0,1:T(8,128)(2,1)}), bf16[2304,2,256]{2,0,1:T(8,128)(2,1)}) %all-gather.7.cloned.1.call-update) | async-done | bytes 2359312 | tf_op jit(solution)/shard_map/all_gather | solution.py:153
  106.7 2.1 fusion.32
  110.4 1.6 convolution_add_fusion.14
  115.0 1.6 convolution_add_fusion.11
  118.3 1.6 convolution_add_fusion.9
  124.4 67.0 %all_gather.18 = bf16[256,80]{1,0:T(8,128)(2,1)S(1)} all-gather(bf16[8,80]{1,0:T(8,128)(2,1)S(1)} %copy-done.36), channel_id=1, replica_groups=mesh['face'=8,'member'=4] {'face','member'}, dimensions={0}, use_global_device_ids=true | all-gather | bytes 42240 | tf_op jit(solution)/shard_map/all_gather | solution.py:154
  191.4 6.1 reshape.813
  197.5 2.6 fusion.4
  204.4 3.9 pad_maximum_fusion.1
  218.7 2.4 convolution_add_fusion
  221.0 3.5 copy.327
  224.6 2.7 multiply_convert_fusion.2
  228.9 1.9 copy.329
  230.8 3.5 all-to-all-start
  234.3 16.0 %all-to-all-done = bf16[2,6,80,256]{2,0,1,3:T(2,128)(2,1)S(1)} async-done(((bf16[2,6,80,256]{2,0,1,3:T(2,128)(2,1)}), bf16[2,6,80,256]{2,0,1,3:T(2,128)(2,1)S(1)}, u32[]{:S(2)}, u32[]{:S(2)}) %all-to-all-start) | async-done | bytes 491552 | tf_op jit(solution)/shard_map/all_to_all | solution.py:171
  250.8 3.1 fusion.2
  255.3 3.5 all-to-all-start.1
  261.1 14.9 %all-to-all-done.1 = bf16[8,6,80,64]{2,3,1,0:T(8,128)(2,1)S(1)} async-done(((bf16[8,6,80,64]{2,3,1,0:T(8,128)(2,1)}), bf16[8,6,80,64]{2,3,1,0:T(8,128)(2,1)S(1)}, u32[]{:S(2)}, u32[]{:S(2)}) %all-to-all-start.1) | async-done | bytes 491552 | tf_op jit(solution)/shard_map/all_to_all | solution.py:176
  276.0 3.5 multiply_convert_fusion.1
  282.5 3.0 scatter-add.44
  285.5 4.8 dynamic-slice_add_fusion
  290.3 18.3 %scatter-add.45 = f32[2,6,18,18,256]{4,2,3,1,0:T(8,128)} dynamic-update-slice(f32[2,6,18,18,256]{4,2,3,1,0:T(8,128)} %scatter-add.44, f32[2,6,16,16,256]{4,2,3,1,0:T(8,128)} %dynamic-slice_add_fusion, s32[]{:T(128)} %constant.394.clone.1, s32[]{:T(128)} %constant.394.clone.1, s32[]{:T(128)} %bitcast.74, s32[]{:T(128)} %bitcast.75, s32[]{:T(128)} %constant.394.clone.1) | dynamic-update-slice | bytes 6291460 | tf_op jit(solution)/shard_map/scatter-add | solution.py:76
  308.5 7.0 add_select_fusion
  315.5 18.3 %scatter-add.46 = f32[2,6,18,18,256]{4,2,3,1,0:T(8,128)} dynamic-update-slice(f32[2,6,18,18,256]{4,2,3,1,0:T(8,128)} %scatter-add.45, f32[2,6,16,16,256]{4,2,3,1,0:T(8,128)} %add_select_fusion, s32[]{:T(128)} %constant.394.clone.1, s32[]{:T(128)} %constant.394.clone.1, s32[]{:T(128)} %bitcast.78, s32[]{:T(128)} %bitcast.79, s32[]{:T(128)} %constant.394.clone.1) | dynamic-update-slice | bytes 6291460 | tf_op jit(solution)/shard_map/scatter-add | solution.py:76
  333.8 5.0 slice_add_fusion.5
  338.7 17.0 %scatter-add.49 = f32[2,6,18,18,256]{4,2,3,1,0:T(8,128)} dynamic-update-slice(f32[2,6,18,18,256]{4,2,3,1,0:T(8,128)} %scatter-add.46, f32[2,6,16,16,256]{4,2,3,1,0:T(8,128)} %slice_add_fusion.5, s32[]{:T(128)} %constant.394.clone.1, s32[]{:T(128)} %constant.394.clone.1, s32[]{:T(128)} %constant.395.clone.1, s32[]{:T(128)} %constant.394.clone.1, s32[]{:T(128)} %constant.394.clone.1) | dynamic-update-slice | bytes 6291460 | tf_op jit(solution)/shard_map/scatter-add | solution.py:76
  355.7 5.0 slice_add_fusion.4
  360.6 16.9 %scatter-add.50 = f32[2,6,18,18,256]{4,2,3,1,0:T(8,128)} dynamic-update-slice(f32[2,6,18,18,256]{4,2,3,1,0:T(8,128)} %scatter-add.49, f32[2,6,16,16,256]{4,2,3,1,0:T(8,128)} %slice_add_fusion.4, s32[]{:T(128)} %constant.394.clone.1, s32[]{:T(128)} %constant.394.clone.1, s32[]{:T(128)} %constant.395.clone.1, s32[]{:T(128)} %constant.395.clone.1, s32[]{:T(128)} %constant.394.clone.1) | dynamic-update-slice | bytes 6291460 | tf_op jit(solution)/shard_map/scatter-add | solution.py:76
  377.6 5.0 slice_add_fusion.3
  382.5 16.9 %scatter-add.51 = f32[2,6,18,18,256]{4,2,3,1,0:T(8,128)} dynamic-update-slice(f32[2,6,18,18,256]{4,2,3,1,0:T(8,128)} %scatter-add.50, f32[2,6,16,16,256]{4,2,3,1,0:T(8,128)} %slice_add_fusion.3, s32[]{:T(128)} %constant.394.clone.1, s32[]{:T(128)} %constant.394.clone.1, s32[]{:T(128)} %constant.395.clone.1, s32[]{:T(128)} %constant.403.clone.1, s32[]{:T(128)} %constant.394.clone.1) | dynamic-update-slice | bytes 6291460 | tf_op jit(solution)/shard_map/scatter-add | solution.py:76
  399.5 5.0 slice_add_fusion.2
  404.4 17.0 %scatter-add.54 = f32[2,6,18,18,256]{4,2,3,1,0:T(8,128)} dynamic-update-slice(f32[2,6,18,18,256]{4,2,3,1,0:T(8,128)} %scatter-add.51, f32[2,6,16,16,256]{4,2,3,1,0:T(8,128)} %slice_add_fusion.2, s32[]{:T(128)} %constant.394.clone.1, s32[]{:T(128)} %constant.394.clone.1, s32[]{:T(128)} %constant.403.clone.1, s32[]{:T(128)} %constant.394.clone.1, s32[]{:T(128)} %constant.394.clone.1) | dynamic-update-slice | bytes 6291460 | tf_op jit(solution)/shard_map/scatter-add | solution.py:76
  421.4 5.0 slice_add_fusion.1
  426.4 16.9 %scatter-add.55 = f32[2,6,18,18,256]{4,2,3,1,0:T(8,128)} dynamic-update-slice(f32[2,6,18,18,256]{4,2,3,1,0:T(8,128)} %scatter-add.54, f32[2,6,16,16,256]{4,2,3,1,0:T(8,128)} %slice_add_fusion.1, s32[]{:T(128)} %constant.394.clone.1, s32[]{:T(128)} %constant.394.clone.1, s32[]{:T(128)} %constant.403.clone.1, s32[]{:T(128)} %constant.395.clone.1, s32[]{:T(128)} %constant.394.clone.1) | dynamic-update-slice | bytes 6291460 | tf_op jit(solution)/shard_map/scatter-add | solution.py:76
  443.3 5.0 slice_add_fusion
  448.3 16.9 %scatter-add.56 = f32[2,6,18,18,256]{4,2,3,1,0:T(8,128)} dynamic-update-slice(f32[2,6,18,18,256]{4,2,3,1,0:T(8,128)} %scatter-add.55, f32[2,6,16,16,256]{4,2,3,1,0:T(8,128)} %slice_add_fusion, s32[]{:T(128)} %constant.394.clone.1, s32[]{:T(128)} %constant.394.clone.1, s32[]{:T(128)} %constant.403.clone.1, s32[]{:T(128)} %constant.403.clone.1, s32[]{:T(128)} %constant.394.clone.1) | dynamic-update-slice | bytes 6291460 | tf_op jit(solution)/shard_map/scatter-add | solution.py:76
  465.2 2.9 convert_element_type.103
  471.1 2.8 convolution_bitcast_fusion.18
  473.9 3.1 fusion.17
  485.7 3.9 slice_convert_fusion
  489.7 13.1 %all-gather.11.cloned.1.call-done = bf16[2,48,4,16,256]{4,3,1,0,2:T(8,128)(2,1)} async-done(((bf16[2,6,4,16,256]{4,3,1,0,2:T(8,128)(2,1)}), bf16[2,48,4,16,256]{4,3,1,0,2:T(8,128)(2,1)}) %all-gather.11.cloned.1.call-update) | async-done | bytes 3145744 | tf_op jit(solution)/shard_map/all_gather | solution.py:187
  502.8 2.3 copy.345
  505.2 3.4 reshape.825
  508.6 2.6 fusion.5
  512.3 2.1 fusion.112
  514.4 5.4 scatter-add.59
  519.9 1.6 fusion.31
  521.5 1.7 slice_add_fusion.6
  523.3 5.5 scatter-add.61
  528.7 5.9 copy.351
  537.1 5.6 scatter-add.64
  542.7 3.1 multiply_convert_fusion
  556.4 76.9 %all-reduce.4.cloned.1.call-done = f32[256,80]{1,0:T(8,128)} async-done(((f32[256,80]{1,0:T(8,128)}), f32[256,80]{1,0:T(8,128)}) %all-reduce.4.cloned.1.call-update) | async-done | bytes 81936
  634.6 102.5 %reduce-scatter.5.cloned.1.call-done = f32[72,256]{1,0:T(8,128)} async-done(((f32[2304,256]{1,0:T(8,128)}), f32[72,256]{1,0:T(8,128)}) %reduce-scatter.5.cloned.1.call-update) | async-done | bytes 73744 | tf_op jit(solution)/shard_map/reduce_scatter | solution.py:183
  737.1 103.9 %reduce-scatter.3.cloned.1.call-done = f32[72,256]{1,0:T(8,128)} async-done(((f32[2304,256]{1,0:T(8,128)}), f32[72,256]{1,0:T(8,128)}) %reduce-scatter.3.cloned.1.call-update) | async-done | bytes 73744 | tf_op jit(solution)/shard_map/reduce_scatter | solution.py:196
  (193 shorter events, 69.2 us)
Async XLA Ops:
  7.2 3.7 copy-start.34
  7.2 4.5 copy-start.38
  7.2 4.8 copy-start.35
  7.2 38.7 %all-gather.5.cloned.1.call-start = ((), (), s32[]{:S(2)}) async-start(), calls=%async_computation.4 | async-start | bytes 3538944 | tf_op jit(solution)/shard_map/all_gather | solution.py:159
  10.8 95.9 %all-gather.7.cloned.1.call-start = ((), (), s32[]{:S(2)}) async-start(), calls=%async_computation.5 | async-start | bytes 2433024 | tf_op jit(solution)/shard_map/all_gather | solution.py:153
  11.6 179.8 %all-gather.9.cloned.1.call-start = ((), (), s32[]{:S(2)}) async-start(), calls=%async_computation.6 | async-start | bytes 3538944 | tf_op jit(solution)/shard_map/all_gather | solution.py:163
  54.8 2.2 copy-start.13
  60.0 55.0 %copy-start.15 = (bf16[2,6,16,16,256]{4,3,2,1,0:T(8,128)(2,1)}, bf16[2,6,16,16,256]{4,3,2,1,0:T(8,128)(2,1)S(1)}, u32[]{:S(2)}) copy-start(bf16[2,6,16,16,256]{4,3,2,1,0:T(8,128)(2,1)S(1)} %get-tuple-element.196) | copy-start | bytes 4718596
  63.6 3.7 copy-start.8
  63.6 3.7 copy-start
  106.7 2.1 copy-start.28
  108.8 1.6 copy-start.27
  110.4 1.6 copy-start.17
  115.0 1.6 copy-start.26
  116.6 1.6 copy-start.25
  118.2 1.6 copy-start.24
  121.4 1.6 copy-start.4
  123.0 1.4 copy-start.36
  204.4 9.6 %copy-start.21 = (bf16[2,6,16,16,256]{4,3,2,1,0:T(8,128)(2,1)}, bf16[2,6,16,16,256]{4,3,2,1,0:T(8,128)(2,1)S(1)}, u32[]{:S(2)}) copy-start(bf16[2,6,16,16,256]{4,3,2,1,0:T(8,128)(2,1)S(1)} %get-tuple-element.191) | copy-start | bytes 4718596
  204.4 12.5 %copy-start.19 = (bf16[2,6,16,16,256]{4,3,2,1,0:T(8,128)(2,1)}, bf16[2,6,16,16,256]{4,3,2,1,0:T(8,128)(2,1)S(1)}, u32[]{:S(2)}) copy-start(bf16[2,6,16,16,256]{4,3,2,1,0:T(8,128)(2,1)S(1)} %get-tuple-element.190) | copy-start | bytes 4718596
  208.3 1.5 copy-start.10
  208.3 2.2 copy-start.2
  210.5 1.7 copy-start.29
  214.0 1.9 copy-start.5
  227.3 1.2 copy-start.7
  228.5 5.8 copy-start.33
  230.8 19.5 %all-to-all-start = ((bf16[2,6,80,256]{2,0,1,3:T(2,128)(2,1)}), bf16[2,6,80,256]{2,0,1,3:T(2,128)(2,1)S(1)}, u32[]{:S(2)}, u32[]{:S(2)}) async-start(bf16[2,6,80,256]{2,0,1,3:T(2,128)(2,1)} %copy.329), calls=%async_computation | async-start | bytes 1572864 | tf_op jit(solution)/shard_map/all_to_all | solution.py:171
  253.9 6.4 copy-start.37
  255.3 20.7 %all-to-all-start.1 = ((bf16[8,6,80,64]{2,3,1,0:T(8,128)(2,1)}), bf16[8,6,80,64]{2,3,1,0:T(8,128)(2,1)S(1)}, u32[]{:S(2)}, u32[]{:S(2)}) async-start(bf16[8,6,80,64]{2,3,1,0:T(8,128)(2,1)} %multiply_convert_fusion.6), calls=%async_computation.1 | async-start | bytes 1572864 | tf_op jit(solution)/shard_map/all_to_all | solution.py:176
  258.8 244.0 %all-gather.11.cloned.1.call-start = ((), (), s32[]{:S(2)}) async-start(), calls=%async_computation.7 | async-start | bytes 3538944 | tf_op jit(solution)/shard_map/all_gather | solution.py:187
  276.0 3.5 copy-start.30
  276.0 3.5 copy-start.11
  465.2 3.4 copy-start.12
  468.1 1.8 copy-start.23
  470.8 162.4 %all-reduce.4.cloned.1.call-start = ((), (), s32[]{:S(2)}) async-start(), calls=%async_computation.10 | async-start | bytes 262144
  473.9 3.1 copy-start.22
  478.4 1.5 copy-start.20
  479.9 1.8 copy-start.3
  485.6 251.4 %reduce-scatter.5.cloned.1.call-start = ((), (), s32[]{:S(2)}) async-start(), calls=%async_computation.9 | async-start | bytes 2433024 | tf_op jit(solution)/shard_map/reduce_scatter | solution.py:183
  489.6 351.4 %reduce-scatter.3.cloned.1.call-start = ((), (), s32[]{:S(2)}) async-start(), calls=%async_computation.8 | async-start | bytes 2433024 | tf_op jit(solution)/shard_map/reduce_scatter | solution.py:196
  512.3 10.9 %copy-start.31 = (f32[2,6,4,16,256]{4,2,3,1,0:T(4,128)}, f32[2,6,4,16,256]{4,2,3,1,0:T(4,128)S(1)}, u32[]{:S(2)}) copy-start(f32[2,6,4,16,256]{4,2,3,1,0:T(4,128)S(1)} %fusion.29) | copy-start | bytes 2359300
  528.7 14.0 %copy-start.6 = (f32[3072,256]{1,0:T(8,128)S(1)}, f32[3072,256]{1,0:T(8,128)}, u32[]{:S(2)}) copy-start(f32[3072,256]{1,0:T(8,128)} %copy-done.4) | copy-start | bytes 9437188
  542.7 3.1 copy-start.9
  547.1 1.4 copy-start.18
  548.5 1.4 copy-start.14
  549.9 1.4 copy-start.16
  551.4 1.7 copy-start.1
  555.0 1.4 copy-start.32
Sparse Core Ops, SparseCore 0:
  11.0 34.8 all-gather.4
  49.5 57.1 all-gather.6
  124.5 31.0 all-gather.8
  471.0 31.8 all-gather.10
  508.8 124.4 all-reduce.3
  638.4 98.5 reduce-scatter.4
  742.3 98.6 reduce-scatter.2
where the time goes:
time: 861 us; the launch traced here: 850 us
  waiting for transfers between devices  396 us (46%)
  local copies, waits for them, and re-layouts  220 us (26%)
  matrix products  99.1 us (12%)
  blocking collectives  67 us (8%)
  other arithmetic  44.6 us (5%)
  between operations  15.6 us (2%)
    scatter-add x9, local copies, waits for them, and re-layouts, transpose_conv(): result.at[:, :, row_off:row_off + height, col_off:col_off + tile_w, :]  141 us
    reduce_scatter x1, waiting for transfers between devices, shards(): lax.psum_scatter(grad_one, ('face', 'member'), scatter_dimension=0, tiled...  104 us
    reduce_scatter x1, waiting for transfers between devices, shards(): lax.psum_scatter(grad_two, ('face', 'member'), scatter_dimension=0, tiled...  102 us
    unnamed x8, waiting for transfers between devices  77 us
    all_gather x1, blocking collectives, shards(): lax.all_gather(head_weight, ('face', 'member'), axis=0, tiled=True)  67 us
    dot_general x9, matrix products, transpose_conv(): lax.dot_general(flat_slope, weight[tap_index * channels:(tap_index + 1) *...  43.1 us
    all_gather x1, waiting for transfers between devices, shards(): lax.all_gather(conv_weights, ('face', 'member'), axis=0, tiled=True)  36.2 us
    all_gather x1, waiting for transfers between devices, shards(): lax.all_gather(split_edges(features), 'face', axis=1, tiled=True)  32.6 us
  transfers between devices with their start and end apart: 9, of which 8 were waited for; matrix products, arithmetic and copies ran while one was open for 11% of the time, Pallas kernels for 0%

commit v1 on v0

--- a/solution.py
+++ b/solution.py
@@ -4,6 +4,18 @@
 from jax.sharding import PartitionSpec as P
 
 smooth_sq = 0.0625
+
+
+def collect(x, axis, dim):
+    ways, here, step = (lax.axis_size(axis), lax.axis_index(axis), x.shape[dim])
+    line, have = (x, 1)
+    while have < ways:
+        line = jnp.concatenate(
+            [line, lax.ppermute(line, axis, [(d, (d - have) % ways) for d in range(ways)])],
+            axis=dim,
+        )
+        have = 2 * have
+    return jnp.roll(line, here * step, axis=dim)
 
 
 def split_edges(grid_field):
@@ -151,7 +163,7 @@
     members, tile_dev, height, tile_w, channels = features.shape
     full_weights, full_head = (
         lax.all_gather(conv_weights, ("face", "member"), axis=0, tiled=True),
-        lax.all_gather(head_weight, ("face", "member"), axis=0, tiled=True),
+        collect(head_weight, ("face", "member"), 0),
     )
     selector, flip_flags = partner_table(
         adjacency, placement_map, lax.axis_index("face") * tile_dev, tile_dev

time: 861 us -> 833 us (0.967)
  blocking collectives: 67 us -> 0 us
  waiting for transfers between devices: 396 us -> 426 us
    all_gather x1 -> x0, blocking collectives: 67 us -> none  [shards(): lax.all_gather(head_weight, ('face', 'member'), axis=0, tiled=True)]
    ppermute x0 -> x5, waiting for transfers between devices: none -> 12.6 us  [collect(): lax.ppermute(line, axis, [(d, (d - have) % ways) for d in range(ways)])]
    all_gather x1, waiting for transfers between devices: 0.01 us -> 12 us  [shards(): lax.all_gather(split_edges(act_one), 'face', axis=1, tiled=True)]
  transfers between devices with their start and end apart: 9 -> 14, of which waited for: 8 -> 14; matrix products, arithmetic and copies ran while one was open for 11% -> 12% of each run, Pallas kernels for 0% -> 0%
where the time goes in v1:
time: 833 us; the launch traced here: 822 us
  waiting for transfers between devices  426 us (51%)
  local copies, waits for them, and re-layouts  218 us (26%)
  matrix products  101 us (12%)
  other arithmetic  46.1 us (6%)
  between operations  15.6 us (2%)
  starting transfers between devices  15.3 us (2%)
    scatter-add x9, local copies, waits for them, and re-layouts, transpose_conv(): result.at[:, :, row_off:row_off + height, col_off:col_off + tile_w, :]  141 us
    reduce_scatter x1, waiting for transfers between devices, shards(): lax.psum_scatter(grad_one, ('face', 'member'), scatter_dimension=0, tiled...  104 us
    reduce_scatter x1, waiting for transfers between devices, shards(): lax.psum_scatter(grad_two, ('face', 'member'), scatter_dimension=0, tiled...  102 us
    unnamed x8, waiting for transfers between devices  77 us
    dot_general x9, matrix products, transpose_conv(): lax.dot_general(flat_slope, weight[tap_index * channels:(tap_index + 1) *...  43 us
    all_gather x1, waiting for transfers between devices, shards(): lax.all_gather(conv_weights, ('face', 'member'), axis=0, tiled=True)  36.2 us
    all_gather x1, waiting for transfers between devices, shards(): lax.all_gather(split_edges(features), 'face', axis=1, tiled=True)  32.6 us
    dot_general x18, matrix products, convolve(): jnp.dot(window.reshape(-1, channels), weight[tap_index * channels:(tap_in...  22.1 us
  transfers between devices with their start and end apart: 14, of which 14 were waited for; matrix products, arithmetic and copies ran while one was open for 12% of the time, Pallas kernels for 0%

profile of v1, /device:TPU:0, one launch (start us, length us, event | category | flops | bytes accessed | tf_op | source)
XLA Modules:
  0.0 822.0 jit_solution(10013245279261809047)
XLA Ops:
  13.3 32.6 %all-gather.5.cloned.1.call-done = bf16[2,48,4,16,256]{4,3,1,0,2:T(8,128)(2,1)} async-done(((bf16[2,6,4,16,256]{4,3,1,0,2:T(8,128)(2,1)}), bf16[2,48,4,16,256]{4,3,1,0,2:T(8,128)(2,1)}) %all-gather.5.cloned.1.call-update) | async-done | bytes 3145744 | tf_op jit(solution)/shard_map/all_gather | solution.py:171
  45.9 2.3 copy.341
  48.3 3.4 reshape.811
  51.7 2.6 fusion.3
  57.0 3.0 pad_maximum_fusion.4
  60.0 3.6 pad_maximum_fusion
  63.6 3.7 fusion.112
  67.3 3.2 fusion.111
  70.5 36.2 %all-gather.7.cloned.1.call-done = bf16[2304,2,256]{2,0,1:T(8,128)(2,1)} async-done(((bf16[72,2,256]{2,0,1:T(8,128)(2,1)}), bf16[2304,2,256]{2,0,1:T(8,128)(2,1)}) %all-gather.7.cloned.1.call-update) | async-done | bytes 2359312 | tf_op jit(solution)/shard_map/all_gather | solution.py:165
  106.7 2.1 fusion.32
  124.5 2.9 collective-permute-start
  129.0 4.8 collective-permute-done.1
  133.9 1.8 collective-permute-done.2
  137.3 2.2 collective-permute-done.3
  141.3 2.3 collective-permute-done.4
  143.7 12.0 %all-gather.9.cloned.1.call-done = bf16[2,48,4,16,256]{4,3,2,1,0:T(8,128)(2,1)} async-done(((bf16[2,6,4,16,256]{4,3,2,1,0:T(8,128)(2,1)}), bf16[2,48,4,16,256]{4,3,2,1,0:T(8,128)(2,1)}) %all-gather.9.cloned.1.call-update) | async-done | bytes 3145744 | tf_op jit(solution)/shard_map/all_gather | solution.py:175
  155.7 6.1 reshape.813
  161.8 2.6 fusion.4
  168.7 3.9 pad_maximum_fusion.1
  182.5 2.4 convolution_add_fusion
  184.9 3.5 copy.375
  188.4 3.9 multiply_convert_fusion.2
  192.3 1.9 fusion.10
  194.2 1.9 copy.377
  196.1 5.0 all-to-all-start
  201.2 20.5 %all-to-all-done = bf16[2,6,80,256]{2,0,1,3:T(2,128)(2,1)S(1)} async-done(((bf16[2,6,80,256]{2,0,1,3:T(2,128)(2,1)}), bf16[2,6,80,256]{2,0,1,3:T(2,128)(2,1)S(1)}, u32[]{:S(2)}, u32[]{:S(2)}) %all-to-all-start) | async-done | bytes 491552 | tf_op jit(solution)/shard_map/all_to_all | solution.py:183
  222.1 3.1 fusion.2
  226.6 3.5 all-to-all-start.1
  232.3 17.4 %all-to-all-done.1 = bf16[8,6,80,64]{2,3,1,0:T(8,128)(2,1)S(1)} async-done(((bf16[8,6,80,64]{2,3,1,0:T(8,128)(2,1)}), bf16[8,6,80,64]{2,3,1,0:T(8,128)(2,1)S(1)}, u32[]{:S(2)}, u32[]{:S(2)}) %all-to-all-start.1) | async-done | bytes 491552 | tf_op jit(solution)/shard_map/all_to_all | solution.py:188
  249.9 3.5 multiply_convert_fusion.1
  256.3 3.0 scatter-add.44
  259.3 4.8 dynamic-slice_add_fusion
  264.1 18.3 %scatter-add.45 = f32[2,6,18,18,256]{4,2,3,1,0:T(8,128)} dynamic-update-slice(f32[2,6,18,18,256]{4,2,3,1,0:T(8,128)} %scatter-add.44, f32[2,6,16,16,256]{4,2,3,1,0:T(8,128)} %dynamic-slice_add_fusion, s32[]{:T(128)} %constant.416.clone.1, s32[]{:T(128)} %constant.416.clone.1, s32[]{:T(128)} %bitcast.74, s32[]{:T(128)} %bitcast.75, s32[]{:T(128)} %constant.416.clone.1) | dynamic-update-slice | bytes 6291460 | tf_op jit(solution)/shard_map/scatter-add | solution.py:88
  282.3 6.9 add_select_fusion
  289.2 18.2 %scatter-add.46 = f32[2,6,18,18,256]{4,2,3,1,0:T(8,128)} dynamic-update-slice(f32[2,6,18,18,256]{4,2,3,1,0:T(8,128)} %scatter-add.45, f32[2,6,16,16,256]{4,2,3,1,0:T(8,128)} %add_select_fusion, s32[]{:T(128)} %constant.416.clone.1, s32[]{:T(128)} %constant.416.clone.1, s32[]{:T(128)} %bitcast.78, s32[]{:T(128)} %bitcast.79, s32[]{:T(128)} %constant.416.clone.1) | dynamic-update-slice | bytes 6291460 | tf_op jit(solution)/shard_map/scatter-add | solution.py:88
  307.4 4.9 slice_add_fusion.5
  312.3 17.0 %scatter-add.49 = f32[2,6,18,18,256]{4,2,3,1,0:T(8,128)} dynamic-update-slice(f32[2,6,18,18,256]{4,2,3,1,0:T(8,128)} %scatter-add.46, f32[2,6,16,16,256]{4,2,3,1,0:T(8,128)} %slice_add_fusion.5, s32[]{:T(128)} %constant.416.clone.1, s32[]{:T(128)} %constant.416.clone.1, s32[]{:T(128)} %constant.417.clone.1, s32[]{:T(128)} %constant.416.clone.1, s32[]{:T(128)} %constant.416.clone.1) | dynamic-update-slice | bytes 6291460 | tf_op jit(solution)/shard_map/scatter-add | solution.py:88
  329.3 5.0 slice_add_fusion.4
  334.2 16.9 %scatter-add.50 = f32[2,6,18,18,256]{4,2,3,1,0:T(8,128)} dynamic-update-slice(f32[2,6,18,18,256]{4,2,3,1,0:T(8,128)} %scatter-add.49, f32[2,6,16,16,256]{4,2,3,1,0:T(8,128)} %slice_add_fusion.4, s32[]{:T(128)} %constant.416.clone.1, s32[]{:T(128)} %constant.416.clone.1, s32[]{:T(128)} %constant.417.clone.1, s32[]{:T(128)} %constant.417.clone.1, s32[]{:T(128)} %constant.416.clone.1) | dynamic-update-slice | bytes 6291460 | tf_op jit(solution)/shard_map/scatter-add | solution.py:88
  351.2 5.0 slice_add_fusion.3
  356.1 16.9 %scatter-add.51 = f32[2,6,18,18,256]{4,2,3,1,0:T(8,128)} dynamic-update-slice(f32[2,6,18,18,256]{4,2,3,1,0:T(8,128)} %scatter-add.50, f32[2,6,16,16,256]{4,2,3,1,0:T(8,128)} %slice_add_fusion.3, s32[]{:T(128)} %constant.416.clone.1, s32[]{:T(128)} %constant.416.clone.1, s32[]{:T(128)} %constant.417.clone.1, s32[]{:T(128)} %constant.430.clone.1, s32[]{:T(128)} %constant.416.clone.1) | dynamic-update-slice | bytes 6291460 | tf_op jit(solution)/shard_map/scatter-add | solution.py:88
  373.1 5.0 slice_add_fusion.2
  378.0 17.0 %scatter-add.54 = f32[2,6,18,18,256]{4,2,3,1,0:T(8,128)} dynamic-update-slice(f32[2,6,18,18,256]{4,2,3,1,0:T(8,128)} %scatter-add.51, f32[2,6,16,16,256]{4,2,3,1,0:T(8,128)} %slice_add_fusion.2, s32[]{:T(128)} %constant.416.clone.1, s32[]{:T(128)} %constant.416.clone.1, s32[]{:T(128)} %constant.430.clone.1, s32[]{:T(128)} %constant.416.clone.1, s32[]{:T(128)} %constant.416.clone.1) | dynamic-update-slice | bytes 6291460 | tf_op jit(solution)/shard_map/scatter-add | solution.py:88
  395.0 5.0 slice_add_fusion.1
  399.9 16.9 %scatter-add.55 = f32[2,6,18,18,256]{4,2,3,1,0:T(8,128)} dynamic-update-slice(f32[2,6,18,18,256]{4,2,3,1,0:T(8,128)} %scatter-add.54, f32[2,6,16,16,256]{4,2,3,1,0:T(8,128)} %slice_add_fusion.1, s32[]{:T(128)} %constant.416.clone.1, s32[]{:T(128)} %constant.416.clone.1, s32[]{:T(128)} %constant.430.clone.1, s32[]{:T(128)} %constant.417.clone.1, s32[]{:T(128)} %constant.416.clone.1) | dynamic-update-slice | bytes 6291460 | tf_op jit(solution)/shard_map/scatter-add | solution.py:88
  416.9 4.9 slice_add_fusion
  421.8 16.9 %scatter-add.56 = f32[2,6,18,18,256]{4,2,3,1,0:T(8,128)} dynamic-update-slice(f32[2,6,18,18,256]{4,2,3,1,0:T(8,128)} %scatter-add.55, f32[2,6,16,16,256]{4,2,3,1,0:T(8,128)} %slice_add_fusion, s32[]{:T(128)} %constant.416.clone.1, s32[]{:T(128)} %constant.416.clone.1, s32[]{:T(128)} %constant.430.clone.1, s32[]{:T(128)} %constant.430.clone.1, s32[]{:T(128)} %constant.416.clone.1) | dynamic-update-slice | bytes 6291460 | tf_op jit(solution)/shard_map/scatter-add | solution.py:88
  438.8 2.9 convert_element_type.103
  444.7 2.8 convolution_bitcast_fusion.18
  447.5 3.2 fusion.17
  459.2 3.9 slice_convert_fusion
  463.2 11.6 %all-gather.11.cloned.1.call-done = bf16[2,48,4,16,256]{4,3,1,0,2:T(8,128)(2,1)} async-done(((bf16[2,6,4,16,256]{4,3,1,0,2:T(8,128)(2,1)}), bf16[2,48,4,16,256]{4,3,1,0,2:T(8,128)(2,1)}) %all-gather.11.cloned.1.call-update) | async-done | bytes 3145744 | tf_op jit(solution)/shard_map/all_gather | solution.py:199
  474.8 2.3 copy.393
  477.2 3.4 reshape.825
  480.6 2.6 fusion.5
  484.4 2.1 fusion.116
  486.5 5.5 scatter-add.59
  495.3 5.5 scatter-add.61
  500.7 5.9 copy.399
  509.1 5.7 scatter-add.64
  514.8 3.1 multiply_convert_fusion
  528.4 76.9 %all-reduce.4.cloned.1.call-done = f32[256,80]{1,0:T(8,128)} async-done(((f32[256,80]{1,0:T(8,128)}), f32[256,80]{1,0:T(8,128)}) %all-reduce.4.cloned.1.call-update) | async-done | bytes 81936
  606.6 102.5 %reduce-scatter.5.cloned.1.call-done = f32[72,256]{1,0:T(8,128)} async-done(((f32[2304,256]{1,0:T(8,128)}), f32[72,256]{1,0:T(8,128)}) %reduce-scatter.5.cloned.1.call-update) | async-done | bytes 73744 | tf_op jit(solution)/shard_map/reduce_scatter | solution.py:195
  709.1 103.9 %reduce-scatter.3.cloned.1.call-done = f32[72,256]{1,0:T(8,128)} async-done(((f32[2304,256]{1,0:T(8,128)}), f32[72,256]{1,0:T(8,128)}) %reduce-scatter.3.cloned.1.call-update) | async-done | bytes 73744 | tf_op jit(solution)/shard_map/reduce_scatter | solution.py:208
  (206 shorter events, 82.0 us)
Async XLA Ops:
  7.2 3.7 copy-start.33
  7.2 4.5 copy-start.37
  7.2 4.7 copy-start.34
  7.2 38.7 %all-gather.5.cloned.1.call-start = ((), (), s32[]{:S(2)}) async-start(), calls=%async_computation.4 | async-start | bytes 3538944 | tf_op jit(solution)/shard_map/all_gather | solution.py:171
  10.8 95.9 %all-gather.7.cloned.1.call-start = ((), (), s32[]{:S(2)}) async-start(), calls=%async_computation.5 | async-start | bytes 2433024 | tf_op jit(solution)/shard_map/all_gather | solution.py:165
  11.6 144.1 %all-gather.9.cloned.1.call-start = ((), (), s32[]{:S(2)}) async-start(), calls=%async_computation.6 | async-start | bytes 3538944 | tf_op jit(solution)/shard_map/all_gather | solution.py:175
  54.8 2.2 copy-start.12
  60.0 55.0 %copy-start.14 = (bf16[2,6,16,16,256]{4,3,2,1,0:T(8,128)(2,1)}, bf16[2,6,16,16,256]{4,3,2,1,0:T(8,128)(2,1)S(1)}, u32[]{:S(2)}) copy-start(bf16[2,6,16,16,256]{4,3,2,1,0:T(8,128)(2,1)S(1)} %get-tuple-element.196) | copy-start | bytes 4718596
  63.6 3.7 copy-start.7
  63.6 3.7 copy-start
  106.7 2.1 copy-start.27
  108.8 1.6 copy-start.26
  110.4 1.6 copy-start.16
  115.0 1.6 copy-start.25
  116.6 1.6 copy-start.24
  118.3 1.6 copy-start.23
  121.4 1.6 copy-start.4
  123.0 1.3 copy-start.35
  124.5 4.4 collective-permute-start
  128.9 4.8 collective-permute-start.1
  133.8 1.9 collective-permute-start.2
  135.8 3.8 collective-permute-start.3
  139.7 3.8 collective-permute-start.4
  168.7 9.1 %copy-start.20 = (bf16[2,6,16,16,256]{4,3,2,1,0:T(8,128)(2,1)}, bf16[2,6,16,16,256]{4,3,2,1,0:T(8,128)(2,1)S(1)}, u32[]{:S(2)}) copy-start(bf16[2,6,16,16,256]{4,3,2,1,0:T(8,128)(2,1)S(1)} %get-tuple-element.191) | copy-start | bytes 4718596
  168.7 11.9 %copy-start.18 = (bf16[2,6,16,16,256]{4,3,2,1,0:T(8,128)(2,1)}, bf16[2,6,16,16,256]{4,3,2,1,0:T(8,128)(2,1)S(1)}, u32[]{:S(2)}) copy-start(bf16[2,6,16,16,256]{4,3,2,1,0:T(8,128)(2,1)S(1)} %get-tuple-element.190) | copy-start | bytes 4718596
  172.6 1.5 copy-start.2
  172.6 2.7 copy-start.9
  174.1 1.9 copy-start.28
  177.8 1.9 copy-start.5
  192.3 8.8 %copy-start.32 = (bf16[6,80,64]{1,2,0:T(8,128)(2,1)S(1)}, bf16[6,80,64]{1,2,0:T(8,128)(2,1)}, u32[]{:S(2)}) copy-start(bf16[6,80,64]{1,2,0:T(8,128)(2,1)} %param.33) | copy-start | bytes 184324
  196.1 25.6 %all-to-all-start = ((bf16[2,6,80,256]{2,0,1,3:T(2,128)(2,1)}), bf16[2,6,80,256]{2,0,1,3:T(2,128)(2,1)S(1)}, u32[]{:S(2)}, u32[]{:S(2)}) async-start(bf16[2,6,80,256]{2,0,1,3:T(2,128)(2,1)} %copy.377), calls=%async_computation | async-start | bytes 1572864 | tf_op jit(solution)/shard_map/all_to_all | solution.py:183
  225.2 6.4 copy-start.36
  226.6 23.1 %all-to-all-start.1 = ((bf16[8,6,80,64]{2,3,1,0:T(8,128)(2,1)}), bf16[8,6,80,64]{2,3,1,0:T(8,128)(2,1)S(1)}, u32[]{:S(2)}, u32[]{:S(2)}) async-start(bf16[8,6,80,64]{2,3,1,0:T(8,128)(2,1)} %multiply_convert_fusion.6), calls=%async_computation.1 | async-start | bytes 1572864 | tf_op jit(solution)/shard_map/all_to_all | solution.py:188
  230.1 244.7 %all-gather.11.cloned.1.call-start = ((), (), s32[]{:S(2)}) async-start(), calls=%async_computation.7 | async-start | bytes 3538944 | tf_op jit(solution)/shard_map/all_gather | solution.py:199
  249.8 3.6 copy-start.29
  249.8 3.6 copy-start.10
  438.8 3.4 copy-start.11
  441.7 1.9 copy-start.22
  444.4 160.9 %all-reduce.4.cloned.1.call-start = ((), (), s32[]{:S(2)}) async-start(), calls=%async_computation.10 | async-start | bytes 262144
  447.5 3.2 copy-start.21
  452.0 1.4 copy-start.19
  453.4 1.8 copy-start.3
  459.2 249.9 %reduce-scatter.5.cloned.1.call-start = ((), (), s32[]{:S(2)}) async-start(), calls=%async_computation.9 | async-start | bytes 2433024 | tf_op jit(solution)/shard_map/reduce_scatter | solution.py:195
  463.2 349.9 %reduce-scatter.3.cloned.1.call-start = ((), (), s32[]{:S(2)}) async-start(), calls=%async_computation.8 | async-start | bytes 2433024 | tf_op jit(solution)/shard_map/reduce_scatter | solution.py:208
  484.3 10.9 %copy-start.30 = (f32[2,6,4,16,256]{4,2,3,1,0:T(4,128)}, f32[2,6,4,16,256]{4,2,3,1,0:T(4,128)S(1)}, u32[]{:S(2)}) copy-start(f32[2,6,4,16,256]{4,2,3,1,0:T(4,128)S(1)} %fusion.29) | copy-start | bytes 2359300
  500.7 14.0 %copy-start.6 = (f32[3072,256]{1,0:T(8,128)S(1)}, f32[3072,256]{1,0:T(8,128)}, u32[]{:S(2)}) copy-start(f32[3072,256]{1,0:T(8,128)} %copy-done.4) | copy-start | bytes 9437188
  514.8 3.1 copy-start.8
  519.1 1.4 copy-start.17
  520.6 1.4 copy-start.13
  522.0 1.4 copy-start.15
  523.4 1.7 copy-start.1
  527.0 1.4 copy-start.31
Sparse Core Ops, SparseCore 0:
  11.0 34.8 all-gather.4
  49.5 57.1 all-gather.6
  124.5 31.2 all-gather.8
  444.5 30.2 all-gather.10
  480.8 124.4 all-reduce.3
  610.5 98.5 reduce-scatter.4
  714.4 98.6 reduce-scatter.2
